TPU v7x, 512 devices: a whole 4x4x16 slice. The times are simulated.
512 devices in a mesh: occ: 8 (over x_lo, y), aux: 64 (over z, x_hi, core).
Axes of the slice: x: 4 (x_hi: 2, x_lo: 2; x = x_hi * 2 + x_lo), y: 4, z: 16, core: 2. Of those that a mesh axis runs over, the one named last changes fastest.
Arguments:
- factors: float32 [8, 640, 24576], P('occ', None, 'aux'), may hold values from -1.75 to 1.75
- occ_energy: float32 [32], replicated, may hold values from -1.5 to -0.3
- vir_energy: float32 [640], replicated, may hold values from 0.2 to 4
- orbital: int32 [8], replicated, may hold values from 0 to 31
- vir_index: int32 [640], replicated, may hold values from 0 to 639, each once
Outputs:
- density: float32 [8, 640, 24576], P('occ', None, 'aux')
Inputs may be any that keep to these rules, and one draw needn't show every extreme that they name: `vir_index`: each virtual's row appears once.
All inputs are finite; a program needn't handle non-finite values.
Results may differ from a plain program's by a relative error of at most 0.0001.
Values sent between devices are 32-bit elements; how exact they have to be, the bound alone decides.
No kernel may reach another device: no remote copies, remote signals or barrier semaphores. Data moves between devices by JAX's collectives and lax.ppermute only.
A program may use at most 64 MiB of HBM per device.

v0:
```python
import jax
import jax.numpy as jnp
from jax import lax
from jax.sharding import PartitionSpec as P

highest = lax.Precision.HIGHEST


def passed_along(value, axis, steps):
    count = lax.axis_size(axis)
    pairs = [(source, (source + steps) % count) for source in range(count)]
    return lax.ppermute(value, axis, pairs)


def product(left, right):
    return jnp.dot(left, right, precision=highest, preferred_element_type=jnp.float32)


def contract_rows(left, right):
    return lax.dot_general(
        left, right, (((0,), (0,)), ((), ())), precision=highest, preferred_element_type=jnp.float32
    )


def contract_cols(left, right):
    return lax.dot_general(
        left, right, (((1,), (1,)), ((), ())), precision=highest, preferred_element_type=jnp.float32
    )


def table_pick(table, indices):
    matches = indices[:, None] == jnp.arange(table.shape[0], dtype=jnp.int32)[None, :]
    return jnp.sum(jnp.where(matches, table[None, :], 0.0), axis=1)


def scalar_pick(values, position):
    matches = jnp.arange(values.shape[0], dtype=jnp.int32) == position
    return jnp.sum(jnp.where(matches, values, 0.0))


def denominator_for(energy_first, energy_second, virtual_energy):
    return energy_first + energy_second - virtual_energy[:, None] - virtual_energy[None, :]


def full_terms(amplitude, local_factor, partner):
    return (product(amplitude, partner), contract_rows(amplitude, local_factor))


def pair_terms(partial_value, denominator, local_factor, partner):
    summed = lax.psum(partial_value, "aux")
    return full_terms(summed / denominator, local_factor, partner)


def body(factors, occ_energy, vir_energy, orbital, vir_index):
    local_factor = factors[0]
    group_index = lax.axis_index("occ")
    group_count = lax.axis_size("occ")
    virtual_energy = table_pick(vir_energy, vir_index)
    orbital_energy = table_pick(occ_energy, orbital)
    energy_self = scalar_pick(orbital_energy, group_index)
    energy_near = scalar_pick(orbital_energy, (group_index + 1) % group_count)
    energy_far = scalar_pick(orbital_energy, (group_index + 3) % group_count)
    near_denominator = denominator_for(energy_self, energy_near, virtual_energy)
    far_denominator = denominator_for(energy_self, energy_far, virtual_energy)
    near_partner = passed_along(local_factor, "occ", -1)
    far_partner = passed_along(local_factor, "occ", -3)
    near_partial = contract_cols(local_factor, near_partner)
    far_partial = contract_cols(local_factor, far_partner)
    near_terms = pair_terms(near_partial, near_denominator, local_factor, near_partner)
    far_terms = pair_terms(far_partial, far_denominator, local_factor, far_partner)
    near_back = passed_along(near_terms[1], "occ", 1)
    far_back = passed_along(far_terms[1], "occ", 3)
    totals = near_terms[0] + far_terms[0] + near_back + far_back
    return totals[None]


def solution(mesh):
    return jax.shard_map(
        body,
        mesh=mesh,
        in_specs=(P("occ", None, "aux"), P(), P(), P(), P()),
        out_specs=P("occ", None, "aux"),
        check_vma=False,
    )
```

profile of v0, /device:TPU:4, one launch (start us, length us, event | category | flops | bytes accessed | tf_op | source)
XLA Modules:
  0.0 659.6 jit_solution(6755391278710232299)
XLA Ops:
  6.5 0.0 all-reduce.3.cloned.1.call-start
  6.5 4.2 collective-permute-start.1
  10.8 3.6 collective-permute-start
  14.4 19.2 %collective-permute-done.1 = f32[640,384]{1,0:T(8,128)S(1)} collective-permute-done((f32[640,384]{1,0:T(8,128)}, f32[640,384]{1,0:T(8,128)S(1)}, u32[]{:S(2)}, u32[]{:S(2)}) %collective-permute-start.1) | collective-permute-done | bytes 983072 | tf_op jit(solution)/shard_map/ppermute | solution.py:12
  33.5 5.4 fusion.11
  38.9 14.2 %collective-permute-done = f32[640,384]{1,0:T(8,128)S(1)} collective-permute-done((f32[640,384]{1,0:T(8,128)}, f32[640,384]{1,0:T(8,128)S(1)}, u32[]{:S(2)}, u32[]{:S(2)}) %collective-permute-start) | collective-permute-done | bytes 983072 | tf_op jit(solution)/shard_map/ppermute | solution.py:12
  53.2 4.2 fusion.13
  57.4 0.0 all-reduce.3.cloned.1.call-update
  57.5 0.6 copy-done.5
  58.1 0.0 copy-done.6
  58.1 0.2 select_reduce_fusion.1
  58.3 0.7 fusion.7
  61.4 0.3 select_reduce_fusion
  61.7 532.0 %all-reduce.3.cloned.1.call-done = (f32[640,640]{1,0:T(8,128)}, f32[640,640]{1,0:T(8,128)}) async-done(((f32[640,640]{1,0:T(8,128)}, f32[640,640]{1,0:T(8,128)}), (f32[640,640]{1,0:T(8,128)}, f32[640,640]{1,0:T(8,128)})) %all-reduce.3.cloned.1.call-update) | async-done | bytes 3276816 | tf_op jit(solution)/shard_map/psum | solution.py:50
  593.8 5.1 fusion.4
  598.9 4.6 collective-permute-start.3
  603.5 0.0 copy-done.3
  603.5 0.0 copy-start.4
  603.5 3.5 fusion.3
  607.0 1.9 collective-permute-start.2
  609.0 3.2 fusion.5
  612.2 13.5 %collective-permute-done.3 = f32[640,384]{1,0:T(8,128)S(1)} collective-permute-done((f32[640,384]{1,0:T(8,128)S(1)}, f32[640,384]{1,0:T(8,128)S(1)}, u32[]{:S(2)}, u32[]{:S(2)}) %collective-permute-start.3) | collective-permute-done | bytes 983072 | tf_op jit(solution)/shard_map/ppermute | solution.py:12
  625.7 22.9 %collective-permute-done.2 = f32[640,384]{1,0:T(8,128)S(1)} collective-permute-done((f32[640,384]{1,0:T(8,128)S(1)}, f32[640,384]{1,0:T(8,128)S(1)}, u32[]{:S(2)}, u32[]{:S(2)}) %collective-permute-start.2) | collective-permute-done | bytes 983072 | tf_op jit(solution)/shard_map/ppermute | solution.py:12
  648.6 4.1 fusion.2
  (11 shorter events, 0.0 us)
Async XLA Ops:
  6.5 587.2 %all-reduce.3.cloned.1.call-start = ((), (), s32[]{:S(2)}) async-start(), calls=%async_computation | async-start | bytes 6553600 | tf_op jit(solution)/shard_map/psum | solution.py:50
  6.5 46.6 %copy-start = (f32[1,640,384]{2,1,0:T(8,128)S(1)}, f32[1,640,384]{2,1,0:T(8,128)}, u32[]{:S(2)}) copy-start(f32[1,640,384]{2,1,0:T(8,128)} %param.5) | copy-start | bytes 2949124
  6.5 27.0 %collective-permute-start.1 = (f32[640,384]{1,0:T(8,128)}, f32[640,384]{1,0:T(8,128)S(1)}, u32[]{:S(2)}, u32[]{:S(2)}) collective-permute-start(f32[640,384]{1,0:T(8,128)} %bitcast.15), channel_id=1, source_target_pairs={{0,320},{64,384},{128,448},{192,0},{256,64},{320,128},{384,192},{4... | collective-permute-start | bytes 2949128 | tf_op jit(solution)/shard_map/ppermute | solution.py:12
  10.8 42.4 %collective-permute-start = (f32[640,384]{1,0:T(8,128)}, f32[640,384]{1,0:T(8,128)S(1)}, u32[]{:S(2)}, u32[]{:S(2)}) collective-permute-start(f32[640,384]{1,0:T(8,128)} %bitcast.16), channel_id=1, source_target_pairs={{0,448},{64,0},{128,64},{192,128},{256,192},{320,256},{384,320},{4... | collective-permute-start | bytes 2949128 | tf_op jit(solution)/shard_map/ppermute | solution.py:12
  57.4 0.7 copy-start.5
  57.4 0.7 copy-start.6
  57.4 3.9 copy-start.1
  57.4 4.0 copy-start.2
  593.7 9.7 %copy-start.3 = (f32[640,640]{1,0:T(8,128)S(1)}, f32[640,640]{1,0:T(8,128)}, u32[]{:S(2)}) copy-start(f32[640,640]{1,0:T(8,128)} %get-tuple-element.9) | copy-start | bytes 4915204
  598.9 26.8 %collective-permute-start.3 = (f32[640,384]{1,0:T(8,128)S(1)}, f32[640,384]{1,0:T(8,128)S(1)}, u32[]{:S(2)}, u32[]{:S(2)}) collective-permute-start(f32[640,384]{1,0:T(8,128)S(1)} %fusion.4), channel_id=1, source_target_pairs={{0,192},{64,256},{128,320},{192,384},{256,448},{320,0},{384,64},{4... | collective-permute-start | bytes 2949128 | tf_op jit(solution)/shard_map/ppermute | solution.py:12
  603.5 5.5 copy-start.4
  607.0 41.6 %collective-permute-start.2 = (f32[640,384]{1,0:T(8,128)S(1)}, f32[640,384]{1,0:T(8,128)S(1)}, u32[]{:S(2)}, u32[]{:S(2)}) collective-permute-start(f32[640,384]{1,0:T(8,128)S(1)} %fusion.3), channel_id=1, source_target_pairs={{0,64},{64,128},{128,192},{192,256},{256,320},{320,384},{384,448},... | collective-permute-start | bytes 2949128 | tf_op jit(solution)/shard_map/ppermute | solution.py:12
Sparse Core Ops, SparseCore 0:
  57.6 536.1 all-reduce.2
where the time goes:
time: 660 us
  waiting for transfers between devices  602 us (91%)
  matrix products  25.6 us (4%)
  between operations  15.9 us (2%)
  starting transfers between devices  14.3 us (2%)
    psum x1, waiting for transfers between devices, pair_terms(): summed = lax.psum(partial_value, 'aux')  532 us
    ppermute x4, waiting for transfers between devices, passed_along(): return lax.ppermute(value, axis, pairs)  69.8 us
    ppermute x4, starting transfers between devices, passed_along(): return lax.ppermute(value, axis, pairs)  14.3 us
  transfers between devices with their start and end apart: 5, of which 5 were waited for; matrix products, arithmetic and copies ran while one was open for 2% of the time, Pallas kernels for 0%

commit v1 on v0

v1 whole, which is shorter than its diff:
```python
import jax
import jax.numpy as jnp
from jax import lax
from jax.sharding import PartitionSpec as P

XL, Y, Z, XH, CORE = 2, 4, 16, 2, 2
RING = Z // 2

STEPS = (
    (1, 0, 3, 2, 5, 4, 7, 6),
    (7, 2, 1, 4, 3, 6, 5, 0),
    (3, 6, 5, 0, 7, 2, 1, 4),
)
KEEPS = (
    (0, 1, 1, 0, 0, 1, 1, 0),
    (0, 0, 1, 0, 1, 1, 0, 1),
)


def flat(place):
    xl, y, z, xh, core = place
    return (((xl * Y + y) * Z + z) * XH + xh) * CORE + core


def places():
    return [
        (xl, y, z, xh, core)
        for xl in range(XL)
        for y in range(Y)
        for z in range(Z)
        for xh in range(XH)
        for core in range(CORE)
    ]


def partner_z(z, core):
    return z ^ 1 if core == 0 else ((z - 1) ^ 1) + 1 & 15


def partner_xy(xl, y, z):
    return (xl, (y + 1) % Y) if z % 2 == 0 else (1 - xl, (y - 1) % Y)


def beside(place):
    xl, y, z, xh, core = place
    return (xl, y, partner_z(z, core), xh, core)


def across(place):
    xl, y, z, xh, core = place
    return (*partner_xy(xl, y, z), z, xh, core)


def diagonal(place):
    xl, y, z, xh, core = place
    return (*partner_xy(xl, y, z), partner_z(z, core), xh, core)


def other_core(place):
    return (*place[:4], 1 - place[4])


def other_half(place):
    xl, y, z, xh, core = place
    return (xl, y, z, 1 - xh, core)


def ring_partner(stage):
    def partner(place):
        xl, y, z, xh, core = place
        r, parity = z // 2, z % 2
        if core == 0:
            r = STEPS[stage][r]
        else:
            r = -STEPS[stage][-r % RING] % RING
        return (xl, y, 2 * r + parity, xh, core)

    return partner


def fetch(value, source_of):
    return lax.ppermute(value, ("occ", "aux"), [(flat(source_of(p)), flat(p)) for p in places()])


def deliver(value, target_of):
    return lax.ppermute(value, ("occ", "aux"), [(flat(p), flat(target_of(p))) for p in places()])


def dot(left, right, dims):
    return lax.dot_general(left, right, (dims, ((), ())), precision=lax.Precision.HIGH, preferred_element_type=jnp.float32)


def table_pick(table, indices):
    matches = indices[:, None] == jnp.arange(table.shape[0], dtype=jnp.int32)[None, :]
    return jnp.sum(jnp.where(matches, table[None, :], 0.0), axis=1)


def scalar_pick(values, position):
    matches = jnp.arange(values.shape[0], dtype=jnp.int32) == position
    return jnp.sum(jnp.where(matches, values, jnp.zeros_like(values)))


def scattered(value, upper, partner):
    half = value.shape[0] // 2
    low, high = value[:half], value[half:]
    received = fetch(jnp.where(upper, low, high), partner)
    return jnp.where(upper, high, low) + received


def gathered(value, upper, partner):
    received = fetch(value, partner)
    return jnp.concatenate([jnp.where(upper, received, value), jnp.where(upper, value, received)], axis=0)


def body(factors, occ_energy, vir_energy, orbital, vir_index):
    mine = factors[0]
    occ, aux = lax.axis_index("occ"), lax.axis_index("aux")
    core, xh, z = aux % 2, aux // 2 % 2, aux // 4
    xl, y = occ // Y, occ % Y
    near = z % 2 == 0
    partner = jnp.where(near, xl * Y + (y + 1) % Y, (1 - xl) * Y + (y + 3) % Y)
    ring = jnp.where(core == 0, z // 2, -(z // 2) % RING)
    keeps = [scalar_pick(jnp.array(k, jnp.int32), ring) for k in KEEPS]
    halves = [core == 1, xh == 1, keeps[0] == 1, keeps[1] == 1]
    partners = [other_core, other_half, ring_partner(0), ring_partner(1)]

    theirs = fetch(mine, across)
    mine_beside = fetch(mine, beside)
    theirs_beside = fetch(mine, diagonal)

    integrals = dot(mine, theirs, ((1,), (1,))) + dot(mine_beside, theirs_beside, ((1,), (1,)))
    for upper, partner_of in zip(halves, partners):
        integrals = scattered(integrals, upper, partner_of)
    integrals = integrals + fetch(integrals, ring_partner(2))

    rows = integrals.shape[0]
    start = core * 320 + xh * 160 + keeps[0] * 80 + keeps[1] * 40
    virtual = table_pick(vir_energy, vir_index)
    virtual_rows = table_pick(vir_energy, lax.dynamic_slice(vir_index, (start,), (rows,)))
    energy = table_pick(occ_energy, orbital)
    pair_energy = scalar_pick(energy, occ) + scalar_pick(energy, partner)
    amplitude = integrals / (pair_energy - virtual_rows[:, None] - virtual[None, :])

    for upper, partner_of in zip(halves[::-1], partners[::-1]):
        amplitude = gathered(amplitude, upper, partner_of)

    from_diagonal = deliver(dot(amplitude, mine_beside, ((0,), (0,))), diagonal)
    from_across = deliver(dot(amplitude, mine, ((0,), (0,))), across)
    from_beside = deliver(dot(amplitude, theirs_beside, ((1,), (0,))), beside)
    total = dot(amplitude, theirs, ((1,), (0,))) + from_beside + from_across + from_diagonal
    return total[None]


def solution(mesh):
    return jax.shard_map(
        body,
        mesh=mesh,
        in_specs=(P("occ", None, "aux"), P(), P(), P(), P()),
        out_specs=P("occ", None, "aux"),
        check_vma=False,
    )
```

time: 660 us -> 203 us (0.31)
  waiting for transfers between devices: 602 us -> 102 us
  starting transfers between devices: 14.3 us -> 80 us
  matrix products: 25.6 us -> 11.1 us
  between operations: 15.9 us -> 4.34 us
    psum x1 -> x0, waiting for transfers between devices: 532 us -> none  [pair_terms(): summed = lax.psum(partial_value, 'aux')]
    ppermute x4 -> x15, starting transfers between devices: 14.3 us -> 80 us  [the longest x12 63.9 us: fetch(): lax.ppermute(value, ('occ', 'aux'), [(flat(source_of(p)), flat(p)) for p...]
    ppermute x4 -> x15, waiting for transfers between devices: 69.8 us -> 102 us  [the longest x12 74.1 us: fetch(): lax.ppermute(value, ('occ', 'aux'), [(flat(source_of(p)), flat(p)) for p...]
    dot_general x6, matrix products: 25.6 us -> 11.1 us  [dot(): lax.dot_general(left, right, (dims, ((), ())), precision=lax.Precision.HI...]
  transfers between devices with their start and end apart: 5 -> 15, of which waited for: 5 -> 15; matrix products, arithmetic and copies ran while one was open for 2% -> 4% of each run, Pallas kernels for 0% -> 0%
where the time goes in v1:
time: 203 us
  waiting for transfers between devices  102 us (50%)
  starting transfers between devices  80 us (39%)
  matrix products  11.1 us (5%)
  other arithmetic  4.73 us (2%)
  between operations  4.34 us (2%)
    ppermute x12, waiting for transfers between devices, fetch(): lax.ppermute(value, ('occ', 'aux'), [(flat(source_of(p)), flat(p)) for p...  74.1 us
    ppermute x12, starting transfers between devices, fetch(): lax.ppermute(value, ('occ', 'aux'), [(flat(source_of(p)), flat(p)) for p...  63.9 us
    ppermute x3, waiting for transfers between devices, deliver(): lax.ppermute(value, ('occ', 'aux'), [(flat(p), flat(target_of(p))) for p...  28.2 us
    ppermute x3, starting transfers between devices, deliver(): lax.ppermute(value, ('occ', 'aux'), [(flat(p), flat(target_of(p))) for p...  16.1 us
    dot_general x6, matrix products, dot(): lax.dot_general(left, right, (dims, ((), ())), precision=lax.Precision.HI...  11.1 us
  transfers between devices with their start and end apart: 15, of which 15 were waited for; matrix products, arithmetic and copies ran while one was open for 4% of the time, Pallas kernels for 0%

profile of v1, /device:TPU:4, one launch (start us, length us, event | category | flops | bytes accessed | tf_op | source)
XLA Modules:
  0.0 202.7 jit_solution(5014559966556191740)
XLA Ops:
  0.0 3.8 %collective-permute-start.1 = (f32[640,384]{1,0:T(8,128)}, f32[640,384]{1,0:T(8,128)S(1)}, u32[]{:S(2)}, u32[]{:S(2)}) collective-permute-start(f32[640,384]{1,0:T(8,128)} %bitcast.13), channel_id=1, source_target_pairs={{4,0},{61,1},{6,2},{63,3},{0,4},{9,5},{2,6},{11,7},{12,8},{5,9},{1... | collective-permute-start | bytes 2949128 | tf_op jit(solution)/shard_map/ppermute | solution.py:82
  3.8 3.7 %collective-permute-start.2 = (f32[640,384]{1,0:T(8,128)}, f32[640,384]{1,0:T(8,128)S(1)}, u32[]{:S(2)}, u32[]{:S(2)}) collective-permute-start(f32[640,384]{1,0:T(8,128)} %bitcast.14), channel_id=1, source_target_pairs={{68,0},{125,1},{70,2},{127,3},{448,4},{457,5},{450,6},{459,7},{76,... | collective-permute-start | bytes 2949128 | tf_op jit(solution)/shard_map/ppermute | solution.py:82
  7.5 3.6 %collective-permute-start = (f32[640,384]{1,0:T(8,128)}, f32[640,384]{1,0:T(8,128)S(1)}, u32[]{:S(2)}, u32[]{:S(2)}) collective-permute-start(f32[640,384]{1,0:T(8,128)} %bitcast.15), channel_id=1, source_target_pairs={{64,0},{65,1},{66,2},{67,3},{452,4},{453,5},{454,6},{455,7},{72,8}... | collective-permute-start | bytes 2949128 | tf_op jit(solution)/shard_map/ppermute | solution.py:82
  11.1 5.1 %collective-permute-done.1 = f32[640,384]{1,0:T(8,128)S(1)} collective-permute-done((f32[640,384]{1,0:T(8,128)}, f32[640,384]{1,0:T(8,128)S(1)}, u32[]{:S(2)}, u32[]{:S(2)}) %collective-permute-start.1) | collective-permute-done | bytes 983072 | tf_op jit(solution)/shard_map/ppermute | solution.py:82
  16.2 19.7 %collective-permute-done.2 = f32[640,384]{1,0:T(8,128)S(1)} collective-permute-done((f32[640,384]{1,0:T(8,128)}, f32[640,384]{1,0:T(8,128)S(1)}, u32[]{:S(2)}, u32[]{:S(2)}) %collective-permute-start.2) | collective-permute-done | bytes 983072 | tf_op jit(solution)/shard_map/ppermute | solution.py:82
  37.5 14.1 %collective-permute-done = f32[640,384]{1,0:T(8,128)S(1)} collective-permute-done((f32[640,384]{1,0:T(8,128)}, f32[640,384]{1,0:T(8,128)S(1)}, u32[]{:S(2)}, u32[]{:S(2)}) %collective-permute-start) | collective-permute-done | bytes 983072 | tf_op jit(solution)/shard_map/ppermute | solution.py:82
  53.4 5.4 %collective-permute-start.3 = (f32[320,640]{1,0:T(8,128)S(1)}, f32[320,640]{1,0:T(8,128)}, u32[]{:S(2)}, u32[]{:S(2)}) collective-permute-start(f32[320,640]{1,0:T(8,128)S(1)} %slice_select_fusion), channel_id=1, source_target_pairs={{1,0},{0,1},{3,2},{2,3},{5,4},{4,5},{7,6},{6,7},{9,8},{8,9},{11,10... | collective-permute-start | bytes 2457608 | tf_op jit(solution)/shard_map/ppermute | solution.py:82
  62.2 4.1 %collective-permute-start.4 = (f32[160,640]{1,0:T(8,128)S(1)}, f32[160,640]{1,0:T(8,128)S(1)}, u32[]{:S(2)}, u32[]{:S(2)}) collective-permute-start(f32[160,640]{1,0:T(8,128)S(1)} %slice_select_fusion.1), channel_id=1, source_target_pairs={{2,0},{3,1},{0,2},{1,3},{6,4},{7,5},{4,6},{5,7},{10,8},{11,9},{8,1... | collective-permute-start | bytes 1228808 | tf_op jit(solution)/shard_map/ppermute | solution.py:82
  70.6 6.7 %collective-permute-done.4 = f32[160,640]{1,0:T(8,128)S(1)} collective-permute-done((f32[160,640]{1,0:T(8,128)S(1)}, f32[160,640]{1,0:T(8,128)S(1)}, u32[]{:S(2)}, u32[]{:S(2)}) %collective-permute-start.4) | collective-permute-done | bytes 409632 | tf_op jit(solution)/shard_map/ppermute | solution.py:82
  77.4 3.8 %collective-permute-start.5 = (f32[80,640]{1,0:T(8,128)S(1)}, f32[80,640]{1,0:T(8,128)S(1)}, u32[]{:S(2)}, u32[]{:S(2)}) collective-permute-start(f32[80,640]{1,0:T(8,128)S(1)} %slice_select_fusion.2), channel_id=1, source_target_pairs={{8,0},{57,1},{10,2},{59,3},{12,4},{61,5},{14,6},{63,7},{0,8},{17,9... | collective-permute-start | bytes 614408 | tf_op jit(solution)/shard_map/ppermute | solution.py:82
  83.3 2.6 %collective-permute-done.5 = f32[80,640]{1,0:T(8,128)S(1)} collective-permute-done((f32[80,640]{1,0:T(8,128)S(1)}, f32[80,640]{1,0:T(8,128)S(1)}, u32[]{:S(2)}, u32[]{:S(2)}) %collective-permute-start.5) | collective-permute-done | bytes 204832 | tf_op jit(solution)/shard_map/ppermute | solution.py:82
  86.0 10.5 %collective-permute-start.6 = (f32[40,640]{1,0:T(8,128)S(1)}, f32[40,640]{1,0:T(8,128)S(1)}, u32[]{:S(2)}, u32[]{:S(2)}) collective-permute-start(f32[40,640]{1,0:T(8,128)S(1)} %slice_select_fusion.3), channel_id=1, source_target_pairs={{56,0},{9,1},{58,2},{11,3},{60,4},{13,5},{62,6},{15,7},{16,8},{1,9... | collective-permute-start | bytes 307208 | tf_op jit(solution)/shard_map/ppermute | solution.py:82
  99.2 7.7 %collective-permute-start.7 = (f32[40,640]{1,0:T(8,128)S(1)}, f32[40,640]{1,0:T(8,128)S(1)}, u32[]{:S(2)}, u32[]{:S(2)}) collective-permute-start(f32[40,640]{1,0:T(8,128)S(1)} %select_add_fusion.3), channel_id=1, source_target_pairs={{24,0},{41,1},{26,2},{43,3},{28,4},{45,5},{30,6},{47,7},{48,8},{33... | collective-permute-start | bytes 307208 | tf_op jit(solution)/shard_map/ppermute | solution.py:82
  107.2 4.3 %collective-permute-done.7 = f32[40,640]{1,0:T(8,128)S(1)} collective-permute-done((f32[40,640]{1,0:T(8,128)S(1)}, f32[40,640]{1,0:T(8,128)S(1)}, u32[]{:S(2)}, u32[]{:S(2)}) %collective-permute-start.7) | collective-permute-done | bytes 102432 | tf_op jit(solution)/shard_map/ppermute | solution.py:82
  111.6 6.5 %collective-permute-start.8 = (f32[40,640]{1,0:T(8,128)S(1)}, f32[40,640]{1,0:T(8,128)S(1)}, u32[]{:S(2)}, u32[]{:S(2)}) collective-permute-start(f32[40,640]{1,0:T(8,128)S(1)} %subtract_divide_fusion), channel_id=1, source_target_pairs={{56,0},{9,1},{58,2},{11,3},{60,4},{13,5},{62,6},{15,7},{16,8},{1,9... | collective-permute-start | bytes 307208 | tf_op jit(solution)/shard_map/ppermute | solution.py:82
  123.2 6.2 %collective-permute-done.9 = f32[80,640]{1,0:T(8,128)S(1)} collective-permute-done((f32[80,640]{1,0:T(8,128)S(1)}, f32[80,640]{1,0:T(8,128)S(1)}, u32[]{:S(2)}, u32[]{:S(2)}) %collective-permute-start.9) | collective-permute-done | bytes 204832 | tf_op jit(solution)/shard_map/ppermute | solution.py:82
  129.4 10.4 %collective-permute-start.10 = (f32[160,640]{1,0:T(8,128)S(1)}, f32[160,640]{1,0:T(8,128)S(1)}, u32[]{:S(2)}, u32[]{:S(2)}) collective-permute-start(f32[160,640]{1,0:T(8,128)S(1)} %pad_maximum_fusion.6), channel_id=1, source_target_pairs={{2,0},{3,1},{0,2},{1,3},{6,4},{7,5},{4,6},{5,7},{10,8},{11,9},{8,1... | collective-permute-start | bytes 1228808 | tf_op jit(solution)/shard_map/ppermute | solution.py:82
  139.9 5.9 %collective-permute-done.10 = f32[160,640]{1,0:T(8,128)S(1)} collective-permute-done((f32[160,640]{1,0:T(8,128)S(1)}, f32[160,640]{1,0:T(8,128)S(1)}, u32[]{:S(2)}, u32[]{:S(2)}) %collective-permute-start.10) | collective-permute-done | bytes 409632 | tf_op jit(solution)/shard_map/ppermute | solution.py:82
  152.2 3.9 %collective-permute-start.13 = (f32[640,384]{1,0:T(8,128)S(1)}, f32[640,384]{1,0:T(8,128)S(1)}, u32[]{:S(2)}, u32[]{:S(2)}) collective-permute-start(f32[640,384]{1,0:T(8,128)S(1)} %fusion.4), channel_id=1, source_target_pairs={{0,64},{1,65},{2,66},{3,67},{4,452},{5,453},{6,454},{7,455},{8,72}... | collective-permute-start | bytes 2949128 | tf_op jit(solution)/shard_map/ppermute | solution.py:86
  158.0 5.1 %collective-permute-start.14 = (f32[640,384]{1,0:T(8,128)S(1)}, f32[640,384]{1,0:T(8,128)S(1)}, u32[]{:S(2)}, u32[]{:S(2)}) collective-permute-start(f32[640,384]{1,0:T(8,128)S(1)} %fusion.3), channel_id=1, source_target_pairs={{0,68},{1,125},{2,70},{3,127},{4,448},{5,457},{6,450},{7,459},{8,7... | collective-permute-start | bytes 2949128 | tf_op jit(solution)/shard_map/ppermute | solution.py:86
  164.7 7.1 %collective-permute-start.12 = (f32[640,384]{1,0:T(8,128)S(1)}, f32[640,384]{1,0:T(8,128)S(1)}, u32[]{:S(2)}, u32[]{:S(2)}) collective-permute-start(f32[640,384]{1,0:T(8,128)S(1)} %fusion.5), channel_id=1, source_target_pairs={{0,4},{1,61},{2,6},{3,63},{4,0},{5,9},{6,2},{7,11},{8,12},{9,5},{1... | collective-permute-start | bytes 2949128 | tf_op jit(solution)/shard_map/ppermute | solution.py:86
  171.8 7.4 %collective-permute-done.13 = f32[640,384]{1,0:T(8,128)S(1)} collective-permute-done((f32[640,384]{1,0:T(8,128)S(1)}, f32[640,384]{1,0:T(8,128)S(1)}, u32[]{:S(2)}, u32[]{:S(2)}) %collective-permute-start.13) | collective-permute-done | bytes 983072 | tf_op jit(solution)/shard_map/ppermute | solution.py:86
  179.3 7.0 %collective-permute-done.14 = f32[640,384]{1,0:T(8,128)S(1)} collective-permute-done((f32[640,384]{1,0:T(8,128)S(1)}, f32[640,384]{1,0:T(8,128)S(1)}, u32[]{:S(2)}, u32[]{:S(2)}) %collective-permute-start.14) | collective-permute-done | bytes 983072 | tf_op jit(solution)/shard_map/ppermute | solution.py:86
  186.3 13.8 %collective-permute-done.12 = f32[640,384]{1,0:T(8,128)S(1)} collective-permute-done((f32[640,384]{1,0:T(8,128)S(1)}, f32[640,384]{1,0:T(8,128)S(1)}, u32[]{:S(2)}, u32[]{:S(2)}) %collective-permute-start.12) | collective-permute-done | bytes 983072 | tf_op jit(solution)/shard_map/ppermute | solution.py:86
  (60 shorter events, 30.0 us)
Async XLA Ops:
  0.0 16.2 %collective-permute-start.1 = (f32[640,384]{1,0:T(8,128)}, f32[640,384]{1,0:T(8,128)S(1)}, u32[]{:S(2)}, u32[]{:S(2)}) collective-permute-start(f32[640,384]{1,0:T(8,128)} %bitcast.13), channel_id=1, source_target_pairs={{4,0},{61,1},{6,2},{63,3},{0,4},{9,5},{2,6},{11,7},{12,8},{5,9},{1... | collective-permute-start | bytes 2949128 | tf_op jit(solution)/shard_map/ppermute | solution.py:82
  3.8 32.0 %collective-permute-start.2 = (f32[640,384]{1,0:T(8,128)}, f32[640,384]{1,0:T(8,128)S(1)}, u32[]{:S(2)}, u32[]{:S(2)}) collective-permute-start(f32[640,384]{1,0:T(8,128)} %bitcast.14), channel_id=1, source_target_pairs={{68,0},{125,1},{70,2},{127,3},{448,4},{457,5},{450,6},{459,7},{76,... | collective-permute-start | bytes 2949128 | tf_op jit(solution)/shard_map/ppermute | solution.py:82
  7.5 44.2 %collective-permute-start = (f32[640,384]{1,0:T(8,128)}, f32[640,384]{1,0:T(8,128)S(1)}, u32[]{:S(2)}, u32[]{:S(2)}) collective-permute-start(f32[640,384]{1,0:T(8,128)} %bitcast.15), channel_id=1, source_target_pairs={{64,0},{65,1},{66,2},{67,3},{452,4},{453,5},{454,6},{455,7},{72,8}... | collective-permute-start | bytes 2949128 | tf_op jit(solution)/shard_map/ppermute | solution.py:82
  11.1 40.6 %copy-start = (f32[1,640,384]{2,1,0:T(8,128)S(1)}, f32[1,640,384]{2,1,0:T(8,128)}, u32[]{:S(2)}) copy-start(f32[1,640,384]{2,1,0:T(8,128)} %param.7) | copy-start | bytes 2949124
  16.2 21.3 %copy-start.4 = (f32[640,384]{1,0:T(8,128)}, f32[640,384]{1,0:T(8,128)S(1)}, u32[]{:S(2)}) copy-start(f32[640,384]{1,0:T(8,128)S(1)} %collective-permute-done.1) | copy-start | bytes 2949124
  53.4 7.5 %collective-permute-start.3 = (f32[320,640]{1,0:T(8,128)S(1)}, f32[320,640]{1,0:T(8,128)}, u32[]{:S(2)}, u32[]{:S(2)}) collective-permute-start(f32[320,640]{1,0:T(8,128)S(1)} %slice_select_fusion), channel_id=1, source_target_pairs={{1,0},{0,1},{3,2},{2,3},{5,4},{4,5},{7,6},{6,7},{9,8},{8,9},{11,10... | collective-permute-start | bytes 2457608 | tf_op jit(solution)/shard_map/ppermute | solution.py:82
  58.8 7.6 %copy-start.11 = (s32[8]{0:T(128)S(1)}, s32[8]{0:T(128)}, u32[]{:S(2)}) copy-start(s32[8]{0:T(128)} %constant.115.clone) | copy-start | bytes 100
  58.8 9.5 %copy-start.10 = (s32[8]{0:T(128)S(1)}, s32[8]{0:T(128)}, u32[]{:S(2)}) copy-start(s32[8]{0:T(128)} %constant.114.clone) | copy-start | bytes 100
  58.8 11.5 %copy-start.7 = (s32[640]{0:T(1024)S(1)}, s32[640]{0:T(1024)}, u32[]{:S(2)}) copy-start(s32[640]{0:T(1024)} %param.11) | copy-start | bytes 7684
  58.9 11.6 %copy-start.8 = (f32[32]{0:T(128)S(1)}, f32[32]{0:T(128)}, u32[]{:S(2)}) copy-start(f32[32]{0:T(128)} %param.8) | copy-start | bytes 388
  58.9 11.6 %copy-start.9 = (s32[8]{0:T(128)S(1)}, s32[8]{0:T(128)}, u32[]{:S(2)}) copy-start(s32[8]{0:T(128)} %param.10) | copy-start | bytes 100
  62.1 21.0 %copy-start.6 = (f32[640]{0:T(1024)S(1)}, f32[640]{0:T(1024)}, u32[]{:S(2)}) copy-start(f32[640]{0:T(1024)} %param.9) | copy-start | bytes 7684
  62.2 15.1 %collective-permute-start.4 = (f32[160,640]{1,0:T(8,128)S(1)}, f32[160,640]{1,0:T(8,128)S(1)}, u32[]{:S(2)}, u32[]{:S(2)}) collective-permute-start(f32[160,640]{1,0:T(8,128)S(1)} %slice_select_fusion.1), channel_id=1, source_target_pairs={{2,0},{3,1},{0,2},{1,3},{6,4},{7,5},{4,6},{5,7},{10,8},{11,9},{8,1... | collective-permute-start | bytes 1228808 | tf_op jit(solution)/shard_map/ppermute | solution.py:82
  77.4 8.6 %collective-permute-start.5 = (f32[80,640]{1,0:T(8,128)S(1)}, f32[80,640]{1,0:T(8,128)S(1)}, u32[]{:S(2)}, u32[]{:S(2)}) collective-permute-start(f32[80,640]{1,0:T(8,128)S(1)} %slice_select_fusion.2), channel_id=1, source_target_pairs={{8,0},{57,1},{10,2},{59,3},{12,4},{61,5},{14,6},{63,7},{0,8},{17,9... | collective-permute-start | bytes 614408 | tf_op jit(solution)/shard_map/ppermute | solution.py:82
  86.0 13.1 %collective-permute-start.6 = (f32[40,640]{1,0:T(8,128)S(1)}, f32[40,640]{1,0:T(8,128)S(1)}, u32[]{:S(2)}, u32[]{:S(2)}) collective-permute-start(f32[40,640]{1,0:T(8,128)S(1)} %slice_select_fusion.3), channel_id=1, source_target_pairs={{56,0},{9,1},{58,2},{11,3},{60,4},{13,5},{62,6},{15,7},{16,8},{1,9... | collective-permute-start | bytes 307208 | tf_op jit(solution)/shard_map/ppermute | solution.py:82
  99.2 12.3 %collective-permute-start.7 = (f32[40,640]{1,0:T(8,128)S(1)}, f32[40,640]{1,0:T(8,128)S(1)}, u32[]{:S(2)}, u32[]{:S(2)}) collective-permute-start(f32[40,640]{1,0:T(8,128)S(1)} %select_add_fusion.3), channel_id=1, source_target_pairs={{24,0},{41,1},{26,2},{43,3},{28,4},{45,5},{30,6},{47,7},{48,8},{33... | collective-permute-start | bytes 307208 | tf_op jit(solution)/shard_map/ppermute | solution.py:82
  111.6 9.1 %collective-permute-start.8 = (f32[40,640]{1,0:T(8,128)S(1)}, f32[40,640]{1,0:T(8,128)S(1)}, u32[]{:S(2)}, u32[]{:S(2)}) collective-permute-start(f32[40,640]{1,0:T(8,128)S(1)} %subtract_divide_fusion), channel_id=1, source_target_pairs={{56,0},{9,1},{58,2},{11,3},{60,4},{13,5},{62,6},{15,7},{16,8},{1,9... | collective-permute-start | bytes 307208 | tf_op jit(solution)/shard_map/ppermute | solution.py:82
  120.7 8.6 %collective-permute-start.9 = (f32[80,640]{1,0:T(8,128)S(1)}, f32[80,640]{1,0:T(8,128)S(1)}, u32[]{:S(2)}, u32[]{:S(2)}) collective-permute-start(f32[80,640]{1,0:T(8,128)S(1)} %pad_maximum_fusion.7), channel_id=1, source_target_pairs={{8,0},{57,1},{10,2},{59,3},{12,4},{61,5},{14,6},{63,7},{0,8},{17,9... | collective-permute-start | bytes 614408 | tf_op jit(solution)/shard_map/ppermute | solution.py:82
  129.4 16.4 %collective-permute-start.10 = (f32[160,640]{1,0:T(8,128)S(1)}, f32[160,640]{1,0:T(8,128)S(1)}, u32[]{:S(2)}, u32[]{:S(2)}) collective-permute-start(f32[160,640]{1,0:T(8,128)S(1)} %pad_maximum_fusion.6), channel_id=1, source_target_pairs={{2,0},{3,1},{0,2},{1,3},{6,4},{7,5},{4,6},{5,7},{10,8},{11,9},{8,1... | collective-permute-start | bytes 1228808 | tf_op jit(solution)/shard_map/ppermute | solution.py:82
  145.9 4.4 %collective-permute-start.11 = (f32[320,640]{1,0:T(8,128)S(1)}, f32[320,640]{1,0:T(8,128)S(1)}, u32[]{:S(2)}, u32[]{:S(2)}) collective-permute-start(f32[320,640]{1,0:T(8,128)S(1)} %pad_maximum_fusion.1), channel_id=1, source_target_pairs={{1,0},{0,1},{3,2},{2,3},{5,4},{4,5},{7,6},{6,7},{9,8},{8,9},{11,10... | collective-permute-start | bytes 2457608 | tf_op jit(solution)/shard_map/ppermute | solution.py:82
  152.2 10.8 %copy-start.3 = (f32[640,384]{1,0:T(8,128)S(1)}, f32[640,384]{1,0:T(8,128)}, u32[]{:S(2)}) copy-start(f32[640,384]{1,0:T(8,128)} %copy-done.2) | copy-start | bytes 2949124
  152.2 27.0 %collective-permute-start.13 = (f32[640,384]{1,0:T(8,128)S(1)}, f32[640,384]{1,0:T(8,128)S(1)}, u32[]{:S(2)}, u32[]{:S(2)}) collective-permute-start(f32[640,384]{1,0:T(8,128)S(1)} %fusion.4), channel_id=1, source_target_pairs={{0,64},{1,65},{2,66},{3,67},{4,452},{5,453},{6,454},{7,455},{8,72}... | collective-permute-start | bytes 2949128 | tf_op jit(solution)/shard_map/ppermute | solution.py:86
  158.0 28.3 %collective-permute-start.14 = (f32[640,384]{1,0:T(8,128)S(1)}, f32[640,384]{1,0:T(8,128)S(1)}, u32[]{:S(2)}, u32[]{:S(2)}) collective-permute-start(f32[640,384]{1,0:T(8,128)S(1)} %fusion.3), channel_id=1, source_target_pairs={{0,68},{1,125},{2,70},{3,127},{4,448},{5,457},{6,450},{7,459},{8,7... | collective-permute-start | bytes 2949128 | tf_op jit(solution)/shard_map/ppermute | solution.py:86
  164.7 35.4 %collective-permute-start.12 = (f32[640,384]{1,0:T(8,128)S(1)}, f32[640,384]{1,0:T(8,128)S(1)}, u32[]{:S(2)}, u32[]{:S(2)}) collective-permute-start(f32[640,384]{1,0:T(8,128)S(1)} %fusion.5), channel_id=1, source_target_pairs={{0,4},{1,61},{2,6},{3,63},{4,0},{5,9},{6,2},{7,11},{8,12},{9,5},{1... | collective-permute-start | bytes 2949128 | tf_op jit(solution)/shard_map/ppermute | solution.py:86
  (3 other events, 11.9 us)

commit v2 on v1

v2 whole, which is shorter than its diff:
```python
import jax
import jax.numpy as jnp
from jax import lax
from jax.sharding import PartitionSpec as P


XL, Y, Z, XH, CORE = 2, 4, 16, 2, 2
SPLITS = (256, 384)
JUMPS = (1, -1, 3, -5)


def flat(place):
    xl, y, z, xh, core = place
    return (((xl * Y + y) * Z + z) * XH + xh) * CORE + core


def places():
    return [
        (xl, y, z, xh, core)
        for xl in range(XL)
        for y in range(Y)
        for z in range(Z)
        for xh in range(XH)
        for core in range(CORE)
    ]


def pair_partner(place):
    xl, y, z, xh, core = place
    return (xl, (y + 1) % Y, z, xh, core) if core == 0 else (1 - xl, (y - 1) % Y, z, xh, core)


def pair_partner_crossed(place):
    return other_core(pair_partner(place))


def other_core(place):
    return (*place[:4], 1 - place[4])


def other_half(place):
    xl, y, z, xh, core = place
    return (xl, y, z, 1 - xh, core)


def hop(stage, r):
    return (r + (JUMPS[stage] if r % 2 == 0 else -JUMPS[stage])) % Z


def ring_partner(stage):
    def partner(place):
        xl, y, z, xh, core = place
        z = hop(stage, z) if core == 0 else -hop(stage, -z % Z) % Z
        return (xl, y, z, xh, core)

    return partner


def keep_bits(stage):
    side, todo = {}, []
    for r in range(Z):
        if r in side:
            continue
        side[r], todo = 0, [r]
        while todo:
            at = todo.pop()
            for later in range(stage, len(JUMPS)):
                to, value = hop(later, at), side[at] ^ (later == stage)
                if to not in side:
                    side[to] = value
                    todo.append(to)
                assert side[to] == value
    return sum(side[r] << r for r in range(Z))


def fetch(value, source_of):
    return lax.ppermute(value, ("occ", "aux"), [(flat(source_of(p)), flat(p)) for p in places()])


def deliver(value, target_of):
    return lax.ppermute(value, ("occ", "aux"), [(flat(p), flat(target_of(p))) for p in places()])


def dot(left, right, dims):
    return lax.dot_general(left, right, (dims, ((), ())), precision=lax.Precision.HIGH, preferred_element_type=jnp.float32)


def table_pick(table, indices):
    matches = indices[:, None] == jnp.arange(table.shape[0], dtype=jnp.int32)[None, :]
    return jnp.sum(jnp.where(matches, table[None, :], 0.0), axis=1)


def scalar_pick(values, position):
    matches = jnp.arange(values.shape[0], dtype=jnp.int32) == position
    return jnp.sum(jnp.where(matches, values, jnp.zeros_like(values)))


def halves(value):
    half = value.shape[0] // 2
    return value[:half], value[half:]


def scattered(parts, upper, partner):
    halved = [halves(v) for v in parts]
    sent = [jnp.where(upper, low, high) for low, high in halved]
    kept = [jnp.where(upper, high, low) for low, high in halved]
    received = fetch(jnp.concatenate(sent, axis=1), partner)
    return jnp.concatenate(kept, axis=1) + received


def joined(value, received, upper):
    return jnp.concatenate([jnp.where(upper, received, value), jnp.where(upper, value, received)], axis=0)


def gathered(value, upper, partner):
    return joined(value, fetch(value, partner), upper)


def body(factors, occ_energy, vir_energy, orbital, vir_index):
    mine = factors[0]
    edges = [sum(SPLITS[:k]) for k in range(len(SPLITS) + 1)]
    spans = list(zip(edges, edges[1:]))
    near = fetch(mine, pair_partner)
    far = [fetch(mine[lo:hi], pair_partner_crossed) for lo, hi in spans]
    theirs = [[near[lo:hi], f] for (lo, hi), f in zip(spans, far)]
    own = [mine, fetch(mine, other_core)]

    occ, aux = lax.axis_index("occ"), lax.axis_index("aux")
    core, xh, z = aux & 1, (aux >> 1) & 1, aux >> 2
    xl, y = occ >> 2, occ & 3
    partner = jnp.where(core == 0, xl * Y + ((y + 1) & 3), (1 - xl) * Y + ((y + 3) & 3))
    ring = jnp.where(core == 0, z, -z & 15)
    keeps = [(jnp.int32(keep_bits(s)) >> ring) & 1 for s in range(3)]
    large = [(keeps[0] == 1, ring_partner(0)), (xh == 1, other_half)]
    small = [(keeps[1] == 1, ring_partner(1)), (keeps[2] == 1, ring_partner(2))]
    start = keeps[0] * 320 + xh * 160 + keeps[1] * 80 + keeps[2] * 40
    rows = 40

    virtual = table_pick(vir_energy, vir_index)
    virtual_rows = table_pick(vir_energy, lax.dynamic_slice(vir_index, (start,), (rows,)))
    energy = table_pick(occ_energy, orbital)
    pair_energy = scalar_pick(energy, occ) + scalar_pick(energy, partner)
    denominator = pair_energy - virtual_rows[:, None] - virtual[None, :]

    kept = [sum(dot(o, t, ((1,), (1,))) for o, t in zip(own, ts)) for ts in theirs]
    for upper, partner_of in large:
        kept = [scattered([k], upper, partner_of) for k in kept]
    for upper, partner_of in small:
        kept = [scattered(kept, upper, partner_of)]
    kept = kept[0] + fetch(kept[0], ring_partner(3))
    kept = kept / denominator
    for upper, partner_of in small[::-1]:
        kept = gathered(kept, upper, partner_of)
    kept = [kept[:, lo:hi] for lo, hi in spans]
    kept = [gathered(k, xh == 1, other_half) for k in kept]
    arrived = [fetch(k, ring_partner(0)) for k in kept]
    full, back = [], []
    for k, a in zip(kept, arrived):
        full.append(joined(k, a, keeps[0] == 1))
        terms = [dot(full[-1], o, ((0,), (0,))) for o in own[::-1]]
        pair = []
        for t, target in zip(terms, (pair_partner_crossed, pair_partner)):
            pair.append(deliver(t, target))
        back.append(pair)
    crossed = sum(dot(k, ts[1], ((1,), (0,))) for k, ts in zip(full, theirs))
    handed = fetch(crossed, other_core)
    straight = sum(dot(k, ts[0], ((1,), (0,))) for k, ts in zip(full, theirs))
    total = straight + handed
    returned = jnp.concatenate([a + b for a, b in back], axis=0)
    return (total + returned)[None]


def solution(mesh):
    return jax.shard_map(
        body,
        mesh=mesh,
        in_specs=(P("occ", None, "aux"), P(), P(), P(), P()),
        out_specs=P("occ", None, "aux"),
        check_vma=False,
    )
```

time: 203 us -> 172 us (0.85)
  the two profiles are of different devices: /device:TPU:4 before, /device:TPU:1 now
where the time goes in v2:
time: 172 us; the launch traced here: 171 us
  starting transfers between devices  84.8 us (49%)
  waiting for transfers between devices  60.1 us (35%)
  matrix products  13.8 us (8%)
  other arithmetic  6.21 us (4%)
  local copies, waits for them, and re-layouts  4.09 us (2%)
  between operations  1.89 us (1%)
    ppermute x18, starting transfers between devices, fetch(): lax.ppermute(value, ('occ', 'aux'), [(flat(source_of(p)), flat(p)) for p...  71.4 us
    ppermute x18, waiting for transfers between devices, fetch(): lax.ppermute(value, ('occ', 'aux'), [(flat(source_of(p)), flat(p)) for p...  50.6 us
    dot_general x12, matrix products, dot(): lax.dot_general(left, right, (dims, ((), ())), precision=lax.Precision.HI...  13.8 us
    ppermute x4, starting transfers between devices, deliver(): lax.ppermute(value, ('occ', 'aux'), [(flat(p), flat(target_of(p))) for p...  13.4 us
    ppermute x4, waiting for transfers between devices, deliver(): lax.ppermute(value, ('occ', 'aux'), [(flat(p), flat(target_of(p))) for p...  9.45 us
    slice x2, local copies, waits for them, and re-layouts, body(): far = [fetch(mine[lo:hi], pair_partner_crossed) for lo, hi in spans]  3.71 us
  transfers between devices with their start and end apart: 22, of which 14 were waited for; matrix products, arithmetic and copies ran while one was open for 13% of the time, Pallas kernels for 0%

profile of v2, /device:TPU:1, one launch (start us, length us, event | category | flops | bytes accessed | tf_op | source)
XLA Modules:
  0.0 170.9 jit_solution(8366048708000390855)
XLA Ops:
  0.0 8.7 %collective-permute-start.1 = (f32[640,384]{1,0:T(8,128)}, f32[640,384]{1,0:T(8,128)S(1)}, u32[]{:S(2)}, u32[]{:S(2)}) collective-permute-start(f32[640,384]{1,0:T(8,128)} %bitcast.23), channel_id=1, source_target_pairs={{1,0},{0,1},{3,2},{2,3},{5,4},{4,5},{7,6},{6,7},{9,8},{8,9},{11,10... | collective-permute-start | bytes 2949128 | tf_op jit(solution)/shard_map/ppermute | solution.py:77
  18.2 9.9 %collective-permute-done.2 = f32[256,384]{1,0:T(8,128)} collective-permute-done((f32[256,384]{1,0:T(8,128)}, f32[256,384]{1,0:T(8,128)}, u32[]{:S(2)}, u32[]{:S(2)}) %collective-permute-start.2) | collective-permute-done | bytes 393248 | tf_op jit(solution)/shard_map/ppermute | solution.py:77
  34.0 5.8 %collective-permute-start.3 = (f32[320,256]{1,0:T(8,128)}, f32[320,256]{1,0:T(8,128)}, u32[]{:S(2)}, u32[]{:S(2)}) collective-permute-start(f32[320,256]{1,0:T(8,128)} %slice_select_fusion.1), channel_id=1, source_target_pairs={{4,0},{61,1},{6,2},{63,3},{0,4},{9,5},{2,6},{11,7},{12,8},{5,9},{1... | collective-permute-start | bytes 983048 | tf_op jit(solution)/shard_map/ppermute | solution.py:77
  42.8 2.6 %collective-permute-start.6 = (f32[320,384]{1,0:T(8,128)}, f32[320,384]{1,0:T(8,128)}, u32[]{:S(2)}, u32[]{:S(2)}) collective-permute-start(f32[320,384]{1,0:T(8,128)} %slice_select_fusion), channel_id=1, source_target_pairs={{4,0},{61,1},{6,2},{63,3},{0,4},{9,5},{2,6},{11,7},{12,8},{5,9},{1... | collective-permute-start | bytes 1474568 | tf_op jit(solution)/shard_map/ppermute | solution.py:77
  47.0 4.6 %collective-permute-start.4 = (f32[160,256]{1,0:T(8,128)S(1)}, f32[160,256]{1,0:T(8,128)S(1)}, u32[]{:S(2)}, u32[]{:S(2)}) collective-permute-start(f32[160,256]{1,0:T(8,128)S(1)} %slice_select_fusion.3), channel_id=1, source_target_pairs={{2,0},{3,1},{0,2},{1,3},{6,4},{7,5},{4,6},{5,7},{10,8},{11,9},{8,1... | collective-permute-start | bytes 491528 | tf_op jit(solution)/shard_map/ppermute | solution.py:77
  55.0 4.4 %collective-permute-start.7 = (f32[160,384]{1,0:T(8,128)S(1)}, f32[160,384]{1,0:T(8,128)S(1)}, u32[]{:S(2)}, u32[]{:S(2)}) collective-permute-start(f32[160,384]{1,0:T(8,128)S(1)} %slice_select_fusion.2), channel_id=1, source_target_pairs={{2,0},{3,1},{0,2},{1,3},{6,4},{7,5},{4,6},{5,7},{10,8},{11,9},{8,1... | collective-permute-start | bytes 737288 | tf_op jit(solution)/shard_map/ppermute | solution.py:77
  59.5 3.9 %collective-permute-done.7 = f32[160,384]{1,0:T(8,128)S(1)} collective-permute-done((f32[160,384]{1,0:T(8,128)S(1)}, f32[160,384]{1,0:T(8,128)S(1)}, u32[]{:S(2)}, u32[]{:S(2)}) %collective-permute-start.7) | collective-permute-done | bytes 245792 | tf_op jit(solution)/shard_map/ppermute | solution.py:77
  70.1 6.7 %collective-permute-start.9 = (f32[40,640]{1,0:T(8,128)S(1)}, f32[40,640]{1,0:T(8,128)S(1)}, u32[]{:S(2)}, u32[]{:S(2)}) collective-permute-start(f32[40,640]{1,0:T(8,128)S(1)} %slice_select_fusion.6), channel_id=1, source_target_pairs={{12,0},{53,1},{14,2},{55,3},{56,4},{17,5},{58,6},{19,7},{20,8},{61... | collective-permute-start | bytes 307208 | tf_op jit(solution)/shard_map/ppermute | solution.py:77
  76.8 3.4 %collective-permute-done.9 = f32[40,640]{1,0:T(8,128)S(1)} collective-permute-done((f32[40,640]{1,0:T(8,128)S(1)}, f32[40,640]{1,0:T(8,128)S(1)}, u32[]{:S(2)}, u32[]{:S(2)}) %collective-permute-start.9) | collective-permute-done | bytes 102432 | tf_op jit(solution)/shard_map/ppermute | solution.py:77
  80.2 3.6 %collective-permute-start.10 = (f32[40,640]{1,0:T(8,128)S(1)}, f32[40,640]{1,0:T(8,128)S(1)}, u32[]{:S(2)}, u32[]{:S(2)}) collective-permute-start(f32[40,640]{1,0:T(8,128)S(1)} %select_add_fusion.4), channel_id=1, source_target_pairs={{44,0},{21,1},{46,2},{23,3},{24,4},{49,5},{26,6},{51,7},{52,8},{29... | collective-permute-start | bytes 307208 | tf_op jit(solution)/shard_map/ppermute | solution.py:77
  84.2 8.5 %collective-permute-done.10 = f32[40,640]{1,0:T(8,128)S(1)} collective-permute-done((f32[40,640]{1,0:T(8,128)S(1)}, f32[40,640]{1,0:T(8,128)S(1)}, u32[]{:S(2)}, u32[]{:S(2)}) %collective-permute-start.10) | collective-permute-done | bytes 102432 | tf_op jit(solution)/shard_map/ppermute | solution.py:77
  92.8 6.3 %collective-permute-start.11 = (f32[40,640]{1,0:T(8,128)S(1)}, f32[40,640]{1,0:T(8,128)S(1)}, u32[]{:S(2)}, u32[]{:S(2)}) collective-permute-start(f32[40,640]{1,0:T(8,128)S(1)} %subtract_divide_fusion), channel_id=1, source_target_pairs={{12,0},{53,1},{14,2},{55,3},{56,4},{17,5},{58,6},{19,7},{20,8},{61... | collective-permute-start | bytes 307208 | tf_op jit(solution)/shard_map/ppermute | solution.py:77
  99.1 3.2 %collective-permute-done.11 = f32[40,640]{1,0:T(8,128)S(1)} collective-permute-done((f32[40,640]{1,0:T(8,128)S(1)}, f32[40,640]{1,0:T(8,128)S(1)}, u32[]{:S(2)}, u32[]{:S(2)}) %collective-permute-start.11) | collective-permute-done | bytes 102432 | tf_op jit(solution)/shard_map/ppermute | solution.py:77
  104.2 4.6 %collective-permute-done.12 = f32[80,640]{1,0:T(8,128)S(1)} collective-permute-done((f32[80,640]{1,0:T(8,128)S(1)}, f32[80,640]{1,0:T(8,128)S(1)}, u32[]{:S(2)}, u32[]{:S(2)}) %collective-permute-start.12) | collective-permute-done | bytes 204832 | tf_op jit(solution)/shard_map/ppermute | solution.py:77
  108.9 4.3 %collective-permute-start.13 = (f32[160,256]{1,0:T(8,128)S(1)}, f32[160,256]{1,0:T(8,128)S(1)}, u32[]{:S(2)}, u32[]{:S(2)}) collective-permute-start(f32[160,256]{1,0:T(8,128)S(1)} %pad_maximum_fusion.15), channel_id=1, source_target_pairs={{2,0},{3,1},{0,2},{1,3},{6,4},{7,5},{4,6},{5,7},{10,8},{11,9},{8,1... | collective-permute-start | bytes 491528 | tf_op jit(solution)/shard_map/ppermute | solution.py:77
  113.2 2.5 %collective-permute-start.15 = (f32[160,384]{1,0:T(8,128)S(1)}, f32[160,384]{1,0:T(8,128)S(1)}, u32[]{:S(2)}, u32[]{:S(2)}) collective-permute-start(f32[160,384]{1,0:T(8,128)S(1)} %pad_maximum_fusion.12), channel_id=1, source_target_pairs={{2,0},{3,1},{0,2},{1,3},{6,4},{7,5},{4,6},{5,7},{10,8},{11,9},{8,1... | collective-permute-start | bytes 737288 | tf_op jit(solution)/shard_map/ppermute | solution.py:77
  118.4 4.3 %collective-permute-done.15 = f32[160,384]{1,0:T(8,128)S(1)} collective-permute-done((f32[160,384]{1,0:T(8,128)S(1)}, f32[160,384]{1,0:T(8,128)S(1)}, u32[]{:S(2)}, u32[]{:S(2)}) %collective-permute-start.15) | collective-permute-done | bytes 245792 | tf_op jit(solution)/shard_map/ppermute | solution.py:77
  126.4 3.1 %collective-permute-start.19 = (f32[256,384]{1,0:T(8,128)S(1)}, f32[256,384]{1,0:T(8,128)S(1)}, u32[]{:S(2)}, u32[]{:S(2)}) collective-permute-start(f32[256,384]{1,0:T(8,128)S(1)} %fusion.11), channel_id=1, source_target_pairs={{0,64},{1,449},{2,66},{3,451},{4,68},{5,453},{6,70},{7,455},{8,72}... | collective-permute-start | bytes 1179656 | tf_op jit(solution)/shard_map/ppermute | solution.py:81
  129.5 4.1 %collective-permute-done.16 = f32[320,384]{1,0:T(8,128)S(1)} collective-permute-done((f32[320,384]{1,0:T(8,128)S(1)}, f32[320,384]{1,0:T(8,128)S(1)}, u32[]{:S(2)}, u32[]{:S(2)}) %collective-permute-start.16) | collective-permute-done | bytes 491552 | tf_op jit(solution)/shard_map/ppermute | solution.py:77
  136.5 8.6 %collective-permute-start.17 = (f32[640,384]{1,0:T(8,128)S(1)}, f32[640,384]{1,0:T(8,128)S(1)}, u32[]{:S(2)}, u32[]{:S(2)}) collective-permute-start(f32[640,384]{1,0:T(8,128)S(1)} %convolution_add_fusion.1), channel_id=1, source_target_pairs={{1,0},{0,1},{3,2},{2,3},{5,4},{4,5},{7,6},{6,7},{9,8},{8,9},{11,10... | collective-permute-start | bytes 2949128 | tf_op jit(solution)/shard_map/ppermute | solution.py:77
  146.2 3.5 %collective-permute-start.21 = (f32[384,384]{1,0:T(8,128)S(1)}, f32[384,384]{1,0:T(8,128)S(1)}, u32[]{:S(2)}, u32[]{:S(2)}) collective-permute-start(f32[384,384]{1,0:T(8,128)S(1)} %fusion.6), channel_id=1, source_target_pairs={{0,64},{1,449},{2,66},{3,451},{4,68},{5,453},{6,70},{7,455},{8,72}... | collective-permute-start | bytes 1769480 | tf_op jit(solution)/shard_map/ppermute | solution.py:81
  150.7 3.5 %collective-permute-start.20 = (f32[384,384]{1,0:T(8,128)S(1)}, f32[384,384]{1,0:T(8,128)S(1)}, u32[]{:S(2)}, u32[]{:S(2)}) collective-permute-start(f32[384,384]{1,0:T(8,128)S(1)} %fusion.7), channel_id=1, source_target_pairs={{0,65},{1,448},{2,67},{3,450},{4,69},{5,452},{6,71},{7,454},{8,73}... | collective-permute-start | bytes 1769480 | tf_op jit(solution)/shard_map/ppermute | solution.py:81
  155.1 3.4 %collective-permute-start.18 = (f32[256,384]{1,0:T(8,128)S(1)}, f32[256,384]{1,0:T(8,128)S(1)}, u32[]{:S(2)}, u32[]{:S(2)}) collective-permute-start(f32[256,384]{1,0:T(8,128)S(1)} %fusion.12), channel_id=1, source_target_pairs={{0,65},{1,448},{2,67},{3,450},{4,69},{5,452},{6,71},{7,454},{8,73}... | collective-permute-start | bytes 1179656 | tf_op jit(solution)/shard_map/ppermute | solution.py:81
  159.6 9.4 %collective-permute-done.18 = f32[256,384]{1,0:T(8,128)S(1)} collective-permute-done((f32[256,384]{1,0:T(8,128)S(1)}, f32[256,384]{1,0:T(8,128)S(1)}, u32[]{:S(2)}, u32[]{:S(2)}) %collective-permute-start.18) | collective-permute-done | bytes 393248 | tf_op jit(solution)/shard_map/ppermute | solution.py:81
  (86 shorter events, 46.2 us)
Async XLA Ops:
  0.0 28.2 %collective-permute-start.1 = (f32[640,384]{1,0:T(8,128)}, f32[640,384]{1,0:T(8,128)S(1)}, u32[]{:S(2)}, u32[]{:S(2)}) collective-permute-start(f32[640,384]{1,0:T(8,128)} %bitcast.23), channel_id=1, source_target_pairs={{1,0},{0,1},{3,2},{2,3},{5,4},{4,5},{7,6},{6,7},{9,8},{8,9},{11,10... | collective-permute-start | bytes 2949128 | tf_op jit(solution)/shard_map/ppermute | solution.py:77
  8.7 23.4 %collective-permute-start = (f32[640,384]{1,0:T(8,128)}, f32[640,384]{1,0:T(8,128)S(1)}, u32[]{:S(2)}, u32[]{:S(2)}) collective-permute-start(f32[640,384]{1,0:T(8,128)} %bitcast.24), channel_id=1, source_target_pairs={{64,0},{449,1},{66,2},{451,3},{68,4},{453,5},{70,6},{455,7},{72,8}... | collective-permute-start | bytes 2949128 | tf_op jit(solution)/shard_map/ppermute | solution.py:77
  12.5 15.7 %collective-permute-start.2 = (f32[256,384]{1,0:T(8,128)}, f32[256,384]{1,0:T(8,128)}, u32[]{:S(2)}, u32[]{:S(2)}) collective-permute-start(f32[256,384]{1,0:T(8,128)} %slice_bitcast_fusion.1), channel_id=1, source_target_pairs={{65,0},{448,1},{67,2},{450,3},{69,4},{452,5},{71,6},{454,7},{73,8}... | collective-permute-start | bytes 1179656 | tf_op jit(solution)/shard_map/ppermute | solution.py:77
  16.3 23.4 %collective-permute-start.5 = (f32[384,384]{1,0:T(8,128)}, f32[384,384]{1,0:T(8,128)S(1)}, u32[]{:S(2)}, u32[]{:S(2)}) collective-permute-start(f32[384,384]{1,0:T(8,128)} %slice_bitcast_fusion), channel_id=1, source_target_pairs={{65,0},{448,1},{67,2},{450,3},{69,4},{452,5},{71,6},{454,7},{73,8}... | collective-permute-start | bytes 1769480 | tf_op jit(solution)/shard_map/ppermute | solution.py:77
  18.2 13.9 %copy-start = (f32[1,640,384]{2,1,0:T(8,128)S(1)}, f32[1,640,384]{2,1,0:T(8,128)}, u32[]{:S(2)}) copy-start(f32[1,640,384]{2,1,0:T(8,128)} %param.5) | copy-start | bytes 2949124
  34.0 11.7 %collective-permute-start.3 = (f32[320,256]{1,0:T(8,128)}, f32[320,256]{1,0:T(8,128)}, u32[]{:S(2)}, u32[]{:S(2)}) collective-permute-start(f32[320,256]{1,0:T(8,128)} %slice_select_fusion.1), channel_id=1, source_target_pairs={{4,0},{61,1},{6,2},{63,3},{0,4},{9,5},{2,6},{11,7},{12,8},{5,9},{1... | collective-permute-start | bytes 983048 | tf_op jit(solution)/shard_map/ppermute | solution.py:77
  42.8 11.1 %collective-permute-start.6 = (f32[320,384]{1,0:T(8,128)}, f32[320,384]{1,0:T(8,128)}, u32[]{:S(2)}, u32[]{:S(2)}) collective-permute-start(f32[320,384]{1,0:T(8,128)} %slice_select_fusion), channel_id=1, source_target_pairs={{4,0},{61,1},{6,2},{63,3},{0,4},{9,5},{2,6},{11,7},{12,8},{5,9},{1... | collective-permute-start | bytes 1474568 | tf_op jit(solution)/shard_map/ppermute | solution.py:77
  47.0 12.5 %collective-permute-start.4 = (f32[160,256]{1,0:T(8,128)S(1)}, f32[160,256]{1,0:T(8,128)S(1)}, u32[]{:S(2)}, u32[]{:S(2)}) collective-permute-start(f32[160,256]{1,0:T(8,128)S(1)} %slice_select_fusion.3), channel_id=1, source_target_pairs={{2,0},{3,1},{0,2},{1,3},{6,4},{7,5},{4,6},{5,7},{10,8},{11,9},{8,1... | collective-permute-start | bytes 491528 | tf_op jit(solution)/shard_map/ppermute | solution.py:77
  55.0 8.4 %collective-permute-start.7 = (f32[160,384]{1,0:T(8,128)S(1)}, f32[160,384]{1,0:T(8,128)S(1)}, u32[]{:S(2)}, u32[]{:S(2)}) collective-permute-start(f32[160,384]{1,0:T(8,128)S(1)} %slice_select_fusion.2), channel_id=1, source_target_pairs={{2,0},{3,1},{0,2},{1,3},{6,4},{7,5},{4,6},{5,7},{10,8},{11,9},{8,1... | collective-permute-start | bytes 737288 | tf_op jit(solution)/shard_map/ppermute | solution.py:77
  59.5 7.9 %copy-start.5 = (f32[640]{0:T(1024)S(1)}, f32[640]{0:T(1024)}, u32[]{:S(2)}) copy-start(f32[640]{0:T(1024)} %param.7) | copy-start | bytes 7684
  63.6 6.5 %collective-permute-start.8 = (f32[80,640]{1,0:T(8,128)S(1)}, f32[80,640]{1,0:T(8,128)S(1)}, u32[]{:S(2)}, u32[]{:S(2)}) collective-permute-start(f32[80,640]{1,0:T(8,128)S(1)} %pad_maximum_fusion.13), channel_id=1, source_target_pairs={{60,0},{5,1},{62,2},{7,3},{8,4},{1,5},{10,6},{3,7},{4,8},{13,9},{6... | collective-permute-start | bytes 614408 | tf_op jit(solution)/shard_map/ppermute | solution.py:77
  70.1 10.1 %collective-permute-start.9 = (f32[40,640]{1,0:T(8,128)S(1)}, f32[40,640]{1,0:T(8,128)S(1)}, u32[]{:S(2)}, u32[]{:S(2)}) collective-permute-start(f32[40,640]{1,0:T(8,128)S(1)} %slice_select_fusion.6), channel_id=1, source_target_pairs={{12,0},{53,1},{14,2},{55,3},{56,4},{17,5},{58,6},{19,7},{20,8},{61... | collective-permute-start | bytes 307208 | tf_op jit(solution)/shard_map/ppermute | solution.py:77
  80.2 12.4 %collective-permute-start.10 = (f32[40,640]{1,0:T(8,128)S(1)}, f32[40,640]{1,0:T(8,128)S(1)}, u32[]{:S(2)}, u32[]{:S(2)}) collective-permute-start(f32[40,640]{1,0:T(8,128)S(1)} %select_add_fusion.4), channel_id=1, source_target_pairs={{44,0},{21,1},{46,2},{23,3},{24,4},{49,5},{26,6},{51,7},{52,8},{29... | collective-permute-start | bytes 307208 | tf_op jit(solution)/shard_map/ppermute | solution.py:77
  92.8 9.5 %collective-permute-start.11 = (f32[40,640]{1,0:T(8,128)S(1)}, f32[40,640]{1,0:T(8,128)S(1)}, u32[]{:S(2)}, u32[]{:S(2)}) collective-permute-start(f32[40,640]{1,0:T(8,128)S(1)} %subtract_divide_fusion), channel_id=1, source_target_pairs={{12,0},{53,1},{14,2},{55,3},{56,4},{17,5},{58,6},{19,7},{20,8},{61... | collective-permute-start | bytes 307208 | tf_op jit(solution)/shard_map/ppermute | solution.py:77
  102.3 6.5 %collective-permute-start.12 = (f32[80,640]{1,0:T(8,128)S(1)}, f32[80,640]{1,0:T(8,128)S(1)}, u32[]{:S(2)}, u32[]{:S(2)}) collective-permute-start(f32[80,640]{1,0:T(8,128)S(1)} %pad_maximum_fusion.14), channel_id=1, source_target_pairs={{60,0},{5,1},{62,2},{7,3},{8,4},{1,5},{10,6},{3,7},{4,8},{13,9},{6... | collective-permute-start | bytes 614408 | tf_op jit(solution)/shard_map/ppermute | solution.py:77
  108.9 7.6 %collective-permute-start.13 = (f32[160,256]{1,0:T(8,128)S(1)}, f32[160,256]{1,0:T(8,128)S(1)}, u32[]{:S(2)}, u32[]{:S(2)}) collective-permute-start(f32[160,256]{1,0:T(8,128)S(1)} %pad_maximum_fusion.15), channel_id=1, source_target_pairs={{2,0},{3,1},{0,2},{1,3},{6,4},{7,5},{4,6},{5,7},{10,8},{11,9},{8,1... | collective-permute-start | bytes 491528 | tf_op jit(solution)/shard_map/ppermute | solution.py:77
  113.2 9.6 %collective-permute-start.15 = (f32[160,384]{1,0:T(8,128)S(1)}, f32[160,384]{1,0:T(8,128)S(1)}, u32[]{:S(2)}, u32[]{:S(2)}) collective-permute-start(f32[160,384]{1,0:T(8,128)S(1)} %pad_maximum_fusion.12), channel_id=1, source_target_pairs={{2,0},{3,1},{0,2},{1,3},{6,4},{7,5},{4,6},{5,7},{10,8},{11,9},{8,1... | collective-permute-start | bytes 737288 | tf_op jit(solution)/shard_map/ppermute | solution.py:77
  116.5 9.0 %collective-permute-start.14 = (f32[320,256]{1,0:T(8,128)S(1)}, f32[320,256]{1,0:T(8,128)S(1)}, u32[]{:S(2)}, u32[]{:S(2)}) collective-permute-start(f32[320,256]{1,0:T(8,128)S(1)} %pad_maximum_fusion.7), channel_id=1, source_target_pairs={{4,0},{61,1},{6,2},{63,3},{0,4},{9,5},{2,6},{11,7},{12,8},{5,9},{1... | collective-permute-start | bytes 983048 | tf_op jit(solution)/shard_map/ppermute | solution.py:77
  122.8 10.8 %collective-permute-start.16 = (f32[320,384]{1,0:T(8,128)S(1)}, f32[320,384]{1,0:T(8,128)S(1)}, u32[]{:S(2)}, u32[]{:S(2)}) collective-permute-start(f32[320,384]{1,0:T(8,128)S(1)} %pad_maximum_fusion.2), channel_id=1, source_target_pairs={{4,0},{61,1},{6,2},{63,3},{0,4},{9,5},{2,6},{11,7},{12,8},{5,9},{1... | collective-permute-start | bytes 1474568 | tf_op jit(solution)/shard_map/ppermute | solution.py:77
  126.4 33.1 %collective-permute-start.19 = (f32[256,384]{1,0:T(8,128)S(1)}, f32[256,384]{1,0:T(8,128)S(1)}, u32[]{:S(2)}, u32[]{:S(2)}) collective-permute-start(f32[256,384]{1,0:T(8,128)S(1)} %fusion.11), channel_id=1, source_target_pairs={{0,64},{1,449},{2,66},{3,451},{4,68},{5,453},{6,70},{7,455},{8,72}... | collective-permute-start | bytes 1179656 | tf_op jit(solution)/shard_map/ppermute | solution.py:81
  136.5 32.7 %collective-permute-start.17 = (f32[640,384]{1,0:T(8,128)S(1)}, f32[640,384]{1,0:T(8,128)S(1)}, u32[]{:S(2)}, u32[]{:S(2)}) collective-permute-start(f32[640,384]{1,0:T(8,128)S(1)} %convolution_add_fusion.1), channel_id=1, source_target_pairs={{1,0},{0,1},{3,2},{2,3},{5,4},{4,5},{7,6},{6,7},{9,8},{8,9},{11,10... | collective-permute-start | bytes 2949128 | tf_op jit(solution)/shard_map/ppermute | solution.py:77
  146.2 22.9 %collective-permute-start.21 = (f32[384,384]{1,0:T(8,128)S(1)}, f32[384,384]{1,0:T(8,128)S(1)}, u32[]{:S(2)}, u32[]{:S(2)}) collective-permute-start(f32[384,384]{1,0:T(8,128)S(1)} %fusion.6), channel_id=1, source_target_pairs={{0,64},{1,449},{2,66},{3,451},{4,68},{5,453},{6,70},{7,455},{8,72}... | collective-permute-start | bytes 1769480 | tf_op jit(solution)/shard_map/ppermute | solution.py:81
  150.7 18.3 %collective-permute-start.20 = (f32[384,384]{1,0:T(8,128)S(1)}, f32[384,384]{1,0:T(8,128)S(1)}, u32[]{:S(2)}, u32[]{:S(2)}) collective-permute-start(f32[384,384]{1,0:T(8,128)S(1)} %fusion.7), channel_id=1, source_target_pairs={{0,65},{1,448},{2,67},{3,450},{4,69},{5,452},{6,71},{7,454},{8,73}... | collective-permute-start | bytes 1769480 | tf_op jit(solution)/shard_map/ppermute | solution.py:81
  155.1 13.9 %collective-permute-start.18 = (f32[256,384]{1,0:T(8,128)S(1)}, f32[256,384]{1,0:T(8,128)S(1)}, u32[]{:S(2)}, u32[]{:S(2)}) collective-permute-start(f32[256,384]{1,0:T(8,128)S(1)} %fusion.12), channel_id=1, source_target_pairs={{0,65},{1,448},{2,67},{3,450},{4,69},{5,452},{6,71},{7,454},{8,73}... | collective-permute-start | bytes 1179656 | tf_op jit(solution)/shard_map/ppermute | solution.py:81
  (7 other events, 32.8 us)
